TPU v7x, 256 devices: a whole 4x4x8 slice. The times are simulated.
256 devices in a mesh: grp: 64 (over y, z, core), sub: 4 (over x).
Axes of the slice: x: 4, y: 4, z: 8, core: 2. Of those that a mesh axis runs over, the one named last changes fastest.
Arguments:
- adj_next: float32 [64, 128, 128, 128], P('grp', 'sub'), may hold values from -4.5 to 4.5
- adj_later: float32 [64, 128, 128, 128], P('grp', 'sub'), may hold values from -2.25 to 2.25
- box_sizes: int32 [64, 2], replicated, may hold values from 64 to 128, as said below
- holder: int32 [64], replicated, may hold values from 0 to 63, as said below
- partner: int32 [64, 2, 4], replicated, may hold values from -1 to 255, as said below
Outputs:
- adj_now: float32 [64, 128, 128, 128], P('grp', 'sub')
- adj_earlier: float32 [64, 128, 128, 128], P('grp', 'sub')
Inputs may be any that keep to these rules, and one draw needn't show every extreme that they name: box_sizes[p] = (Lx, Ly) with 64 <= Lx <= 128 and 64 <= Ly <= 128; some partition has Lx = 128 and Ly = 128, some has Lx = 64, some has Ly = 64. holder names every slot exactly once. The joining is mutual: if partner[p, f, s] = q * 4 + t then partner[q, 1 - f, t] = p * 4 + s, and q differs from p. A face may be joined in part and walled in part; some faces are wholly walls. Over both faces, a partition has at most 3 segments joined to any one other partition, and some pair of partitions has exactly 3.
All inputs are finite; a program needn't handle non-finite values.
Results may differ from a plain program's by a relative error of at most 0.0003.
Values sent between devices are 32-bit elements; how exact they have to be, the bound alone decides.
A program may use at most 128 MiB of HBM per device.

v0:
```python
import jax
import jax.numpy as jnp
from jax import lax
from jax.sharding import PartitionSpec as P

time_step = 0.5
precise = lax.Precision.HIGHEST
stencil_rows = (
    (0, 0, -2, 2, 0, 0),
    (0, 2, -27, 27, -2, 0),
    (-2, 27, -270, 270, -27, 2),
    (2, -27, 270, -270, 27, -2),
    (0, -2, 27, -27, 2, 0),
    (0, 0, 2, -2, 0, 0),
)


def cosine_table(size_cells, length):
    mode_index = jnp.arange(size_cells, dtype=jnp.int32)[:, None]
    cell_index = jnp.arange(size_cells, dtype=jnp.int32)[None, :]
    extent = length.astype(jnp.float32)
    angles = (
        jnp.pi * mode_index.astype(jnp.float32) * (cell_index.astype(jnp.float32) + 0.5) / extent
    )
    scaling = jnp.sqrt(jnp.where(mode_index == 0, 1.0, 2.0).astype(jnp.float32) / extent)
    inside = (mode_index < length) & (cell_index < length)
    return jnp.where(inside, scaling * jnp.cos(angles), jnp.float32(0.0))


def update_factors(len_x, len_y, first_y, count_y, total_x, total_z):
    wave_x = jnp.arange(total_x, dtype=jnp.int32).astype(jnp.float32) / len_x.astype(jnp.float32)
    wave_y = (first_y + jnp.arange(count_y, dtype=jnp.int32)).astype(jnp.float32) / len_y.astype(
        jnp.float32
    )
    wave_z = jnp.arange(total_z, dtype=jnp.int32).astype(jnp.float32) / jnp.float32(total_z)
    angular = jnp.pi * jnp.sqrt(
        wave_x[:, None, None] ** 2 + wave_y[None, :, None] ** 2 + wave_z[None, None, :] ** 2
    )
    two_cos = 2.0 * jnp.cos(angular * time_step)
    source = time_step**2 * jnp.sinc(angular * (time_step / (2.0 * jnp.pi))) ** 2
    return (two_cos, source.astype(jnp.float32))


def plane_inverse(spectral, table_y, table_z):
    physical = jnp.einsum("ly,xlm->xym", table_y, spectral, precision=precise)
    return jnp.einsum("mz,xym->xyz", table_z, physical, precision=precise)


def coupling_terms(own_strips, other_strips):
    weights = jnp.transpose(jnp.asarray(stencil_rows, dtype=jnp.float32)) / 180.0
    low_terms = jnp.einsum(
        "ij,...jw->...iw", weights[3:6, 0:3], other_strips[..., 0, :, :, :], precision=precise
    ) + jnp.einsum(
        "ij,...jw->...iw", weights[3:6, 3:6], own_strips[..., 0, :, :, :], precision=precise
    )
    high_terms = jnp.einsum(
        "ij,...jw->...iw", weights[0:3, 0:3], own_strips[..., 1, :, :, :], precision=precise
    ) + jnp.einsum(
        "ij,...jw->...iw", weights[0:3, 3:6], other_strips[..., 1, :, :, :], precision=precise
    )
    return jnp.stack([low_terms, high_terms], axis=-4)


def to_segments(strip_rows, pieces):
    x_cells, row_count, z_cells = strip_rows.shape
    layered = strip_rows.reshape(x_cells, row_count, pieces, z_cells // pieces)
    return jnp.transpose(layered, (2, 1, 0, 3)).reshape(
        pieces, row_count, x_cells * (z_cells // pieces)
    )


def from_segments(values, x_cells):
    pieces, row_count, flat_width = values.shape
    layered = values.reshape(pieces, row_count, x_cells, flat_width // x_cells)
    return jnp.transpose(layered, (2, 1, 0, 3)).reshape(
        x_cells, row_count, pieces * (flat_width // x_cells)
    )


def local(adj_next, adj_later, box_sizes, holder, partner):
    part_count = holder.shape[0]
    seg_count = partner.shape[2]
    item_count = 2 * seg_count
    my_group = lax.axis_index("grp")
    my_column = lax.axis_index("sub")
    sub_count = lax.axis_size("sub")
    x_local = adj_next.shape[1]
    y_cells = adj_next.shape[2]
    z_cells = adj_next.shape[3]
    x_total = x_local * sub_count
    y_local = y_cells // sub_count
    seg_cells = z_cells // seg_count
    strip_width = x_local * seg_cells
    part_ids = jnp.arange(part_count, dtype=jnp.int32)
    my_part = jnp.sum(jnp.where(holder == my_group, part_ids, 0))
    len_x = box_sizes[my_part, 0]
    len_y = box_sizes[my_part, 1]
    table_x = cosine_table(x_total, len_x)
    table_y = cosine_table(y_cells, len_y)
    table_z = cosine_table(z_cells, jnp.int32(z_cells))
    face_table = jnp.concatenate(
        [table_y[:, 0:3], lax.dynamic_slice_in_dim(table_y, len_y - 3, 3, 1)], axis=1
    )
    two_cos, source = update_factors(len_x, len_y, my_column * y_local, y_local, x_total, z_cells)
    x_global = my_column * x_local + jnp.arange(x_local, dtype=jnp.int32)
    y_index = jnp.arange(y_cells, dtype=jnp.int32)
    inside = ((x_global[:, None, None] < len_x) & (y_index[None, :, None] < len_y)).astype(
        jnp.float32
    )
    link_ids = partner[my_part].reshape(item_count)
    is_wall = link_ids < 0
    safe_links = jnp.maximum(link_ids, 0)
    peer_part = safe_links // seg_count
    peer_seg = safe_links % seg_count
    peer_group = holder[peer_part]
    item_ids = jnp.arange(item_count, dtype=jnp.int32)
    peer_item = (1 - item_ids // seg_count) * seg_count + peer_seg
    x_limit = jnp.minimum(len_x, box_sizes[peer_part, 0])
    column_x = my_column * x_local + jnp.arange(strip_width, dtype=jnp.int32) // seg_cells
    joined = ((column_x[None, :] < x_limit[:, None]) & jnp.logical_not(is_wall)[:, None]).astype(
        jnp.float32
    )
    joined = joined.reshape(2, seg_count, 1, strip_width)

    def reverse_step(current, earlier):
        spectral = jnp.einsum("mz,xyz->xym", table_z, current[0], precision=precise)
        spectral = jnp.einsum("ly,xym->xlm", table_y, spectral, precision=precise)
        spectral = lax.all_to_all(spectral, "sub", split_axis=1, concat_axis=0, tiled=True)
        spectral = jnp.einsum("kx,xlm->klm", table_x, spectral, precision=precise)
        wave_part = jnp.einsum("kx,klm->xlm", table_x, two_cos * spectral, precision=precise)
        force_part = jnp.einsum("kx,klm->xlm", table_x, source * spectral, precision=precise)
        wave_part, force_part = (
            lax.all_to_all(wave_part, "sub", split_axis=0, concat_axis=1, tiled=True),
            lax.all_to_all(force_part, "sub", split_axis=0, concat_axis=1, tiled=True),
        )
        face_rows = plane_inverse(force_part, face_table, table_z)
        wave_part = plane_inverse(wave_part, table_y, table_z)
        low_rows = face_rows[:, 0:3, :]
        high_rows = face_rows[:, 3:6, :]
        own_strips = jnp.concatenate(
            [to_segments(low_rows, seg_count), to_segments(high_rows, seg_count)], axis=0
        )
        everyone = lax.all_gather(own_strips[None], "grp", axis=0, tiled=True)
        everyone = everyone.reshape(part_count * item_count, 3, strip_width)
        other_strips = everyone[peer_group * item_count + peer_item]
        coupled = coupling_terms(
            own_strips.reshape(2, seg_count, 3, strip_width),
            other_strips.reshape(2, seg_count, 3, strip_width),
        )
        coupled = coupled * joined
        result = wave_part - inside * earlier[0]
        result = result.at[:, 0:3, :].add(from_segments(coupled[0], x_local))
        window = lax.dynamic_slice_in_dim(result, len_y - 3, 3, 1)
        result = lax.dynamic_update_slice_in_dim(
            result, window + from_segments(coupled[1], x_local), len_y - 3, 1
        )
        return result[None]

    adj_now = reverse_step(adj_next, adj_later)
    adj_earlier = reverse_step(adj_now, adj_next)
    return (adj_now, adj_earlier)


def solution(mesh):
    return jax.shard_map(
        local,
        mesh=mesh,
        in_specs=(P("grp", "sub", None, None), P("grp", "sub", None, None), P(), P(), P()),
        out_specs=(P("grp", "sub", None, None), P("grp", "sub", None, None)),
        check_vma=False,
    )
```

profile of v0, /device:TPU:9, one launch (start us, length us, event | category | flops | bytes accessed | tf_op | source)
XLA Modules:
  0.0 375.5 jit_solution(16978702654708273522)
XLA Ops:
  7.2 1.3 fusion.194
  10.4 1.3 constant_dynamic-slice_fusion.1
  12.4 0.7 iota_compare_fusion
  13.1 3.8 %fusion.15 = f32[128,32,128]{2,0,1:T(8,128)S(1)} fusion(f32[1,32,128,128]{3,2,1,0:T(8,128)} %param.11, f32[128]{0:T(128)S(1)} %get-tuple-element.45, f32[128]{0:T(128)S(1)} %get-tuple-element.46, f32[128]{0:T(128)S(1)} %get-tuple-element.47, pred[128]{0:T(512)(128)(4,1)S(1)} %iota_compare_fusion.1), kind=kOutput, calls=%fused_computation.27 | convolution fusion | flops 805388288 | bytes 4195968 | tf_op jit(solution)/shard_map/mz,xyz->xym/dot_general | solution.py:126
  16.9 2.1 fusion.32
  19.0 2.0 copy.159
  20.9 4.5 %all-to-all-start = ((f32[32,128,128]{2,0,1:T(8,128)}), f32[32,128,128]{2,0,1:T(8,128)S(1)}, u32[]{:S(2)}, u32[]{:S(2)}) async-start(f32[32,128,128]{2,0,1:T(8,128)} %copy.159), calls=%async_computation | async-start | bytes 4194304 | tf_op jit(solution)/shard_map/all_to_all | solution.py:128
  26.7 24.2 %all-to-all-done = f32[32,128,128]{2,0,1:T(8,128)S(1)} async-done(((f32[32,128,128]{2,0,1:T(8,128)}), f32[32,128,128]{2,0,1:T(8,128)S(1)}, u32[]{:S(2)}, u32[]{:S(2)}) %all-to-all-start) | async-done | bytes 2097184 | tf_op jit(solution)/shard_map/all_to_all | solution.py:128
  51.1 2.2 fusion.91
  53.4 5.3 %fusion.22 = f32[128,32,128]{2,0,1:T(8,128)S(1)} fusion(f32[128,32,128]{2,0,1:T(8,128)S(1)} %fusion.91, f32[128]{0:T(128)S(1)} %multiply_multiply_fusion.5, f32[128,32]{0,1:T(8,128)S(1)} %broadcast_add_fusion, f32[]{:T(128)S(6)} %convert_element_type.81, f32[128]{0:T(128)S(1)} %get-tuple-element.46, f32[128]{0:T(128)S(1)} %get-tuple-element.47, ...), kind=kOutput, calls=%fused_computation.34 | convolution fusion | flops 825311232 | bytes 4212868 | tf_op jit(solution)/shard_map/kx,klm->xlm/dot_general | solution.py:131
  58.7 2.5 copy.169
  61.3 4.4 %all-to-all-start.2 = ((f32[128,32,128]{2,1,0:T(8,128)}), f32[128,32,128]{2,1,0:T(8,128)}, u32[]{:S(2)}, u32[]{:S(2)}) async-start(f32[128,32,128]{2,1,0:T(8,128)} %copy.169), calls=%async_computation.2 | async-start | bytes 4194304 | tf_op jit(solution)/shard_map/all_to_all | solution.py:134
  67.6 22.8 %all-to-all-done.2 = f32[128,32,128]{2,1,0:T(8,128)} async-done(((f32[128,32,128]{2,1,0:T(8,128)}), f32[128,32,128]{2,1,0:T(8,128)}, u32[]{:S(2)}, u32[]{:S(2)}) %all-to-all-start.2) | async-done | bytes 2097184 | tf_op jit(solution)/shard_map/all_to_all | solution.py:134
  90.4 1.8 copy.170
  92.2 1.2 convolution_bitcast_fusion.2
  94.6 0.7 pad_maximum_fusion
  95.3 9.9 %fusion.30 = f32[128,32,128]{2,0,1:T(8,128)S(1)} fusion(f32[128,32,128]{2,0,1:T(8,128)S(1)} %fusion.91, f32[128]{0:T(128)S(1)} %multiply_multiply_fusion.5, f32[128,32]{0,1:T(8,128)S(1)} %broadcast_add_fusion, f32[]{:T(128)S(6)} %convert_element_type.81, f32[128]{0:T(128)S(1)} %get-tuple-element.46, f32[128]{0:T(128)S(1)} %get-tuple-element.47, ...), kind=kOutput, calls=%fused_computation.47 | convolution fusion | flops 807485440 | bytes 4212868 | tf_op jit(solution)/shard_map/kx,klm->xlm/dot_general | solution.py:130
  105.2 2.5 copy.163
  107.7 3.7 all-to-all-start.1
  112.3 0.6 gather_fusion
  113.0 0.7 gather_fusion.2
  113.6 0.6 broadcast_minimum_fusion
  114.3 0.6 fusion.196
  115.1 20.2 %all-to-all-done.1 = f32[128,32,128]{2,1,0:T(8,128)S(1)} async-done(((f32[128,32,128]{2,1,0:T(8,128)}), f32[128,32,128]{2,1,0:T(8,128)S(1)}, u32[]{:S(2)}, u32[]{:S(2)}) %all-to-all-start.1) | async-done | bytes 2097184 | tf_op jit(solution)/shard_map/all_to_all | solution.py:133
  136.5 3.6 fusion.71
  140.1 4.2 %fusion.10 = f32[32,128,128]{2,1,0:T(8,128)S(1)} fusion(f32[1,32,128,128]{3,2,1,0:T(8,128)S(1)} %copy-done.5, f32[32,128,128]{2,1,0:T(8,128)S(1)} %fusion.71, f32[32,128]{1,0:T(8,128)S(1)} %and_convert_fusion.1, f32[128]{0:T(128)S(1)} %get-tuple-element.45, f32[128]{0:T(128)S(1)} %get-tuple-element.46, f32[128]{0:T(128)S(1)} %get-tuple-element.47, ...), kind=kOutput, calls=%fused_computation.21 | convolution fusion | flops 806436864 | bytes 6309504 | tf_op jit(solution)/shard_map/mz,xym->xyz/dot_general | solution.py:46
  144.3 33.9 %all-gather.5.cloned.1.call-done = f32[512,3,1024]{2,0,1:T(8,128)} async-done(((f32[8,3,1024]{2,0,1:T(8,128)}), f32[512,3,1024]{2,0,1:T(8,128)}) %all-gather.5.cloned.1.call-update) | async-done | bytes 6291472 | tf_op jit(solution)/shard_map/all_gather | solution.py:143
  178.2 10.7 %copy.175 = f32[512,3,1024]{2,1,0:T(4,128)} copy(f32[512,3,1024]{2,0,1:T(8,128)} %all-gather.5.cloned.1.call-done) | data formatting | bytes 12582912 | tf_op jit(solution)/shard_map/all_gather | solution.py:143
  189.0 4.0 %gather_fusion.1 = f32[8,3,1024]{2,1,0:T(4,128)S(1)} fusion(f32[512,3,1024]{2,1,0:T(4,128)} %copy.175, s32[1024]{0:T(1024)S(1)} %pad_clamp_fusion), kind=kCustom, calls=%fused_computation.1 | custom fusion | bytes 196640 | tf_op jit(solution)/shard_map/gather | solution.py:145
  195.1 2.3 fusion.84
  197.5 3.4 convolution_bitcast_fusion
  200.9 2.4 copy.187
  203.2 29.8 %all_to_all.108 = f32[32,128,128]{2,0,1:T(8,128)S(1)} all-to-all(f32[32,128,128]{2,0,1:T(8,128)S(1)} %copy.187), channel_id=1, replica_groups=mesh['grp'=64,'sub'=4] {'sub'}, dimensions={1} | all-to-all | bytes 4194304 | tf_op jit(solution)/shard_map/all_to_all | solution.py:128
  233.3 2.2 fusion.89
  235.5 5.3 %fusion.18 = f32[128,32,128]{2,0,1:T(8,128)S(1)} fusion(f32[128,32,128]{2,0,1:T(8,128)S(1)} %fusion.89, f32[128]{0:T(128)S(1)} %multiply_multiply_fusion.5, f32[128,32]{0,1:T(8,128)S(1)} %broadcast_add_fusion, f32[]{:T(128)S(6)} %convert_element_type.81, f32[128]{0:T(128)S(1)} %get-tuple-element.46, f32[128]{0:T(128)S(1)} %get-tuple-element.47, ...), kind=kOutput, calls=%fused_computation.30 | convolution fusion | flops 825311232 | bytes 4212868 | tf_op jit(solution)/shard_map/kx,klm->xlm/dot_general | solution.py:131
  240.9 1.2 copy.197
  242.1 27.2 %all_to_all.109 = f32[128,32,128]{2,1,0:T(8,128)S(1)} all-to-all(f32[128,32,128]{2,1,0:T(8,128)S(1)} %copy.197), channel_id=1, replica_groups=mesh['grp'=64,'sub'=4] {'sub'}, dimensions={0} | all-to-all | bytes 4194304 | tf_op jit(solution)/shard_map/all_to_all | solution.py:134
  269.5 1.2 convolution_bitcast_fusion.1
  271.9 0.7 pad_maximum_fusion.1
  272.6 10.1 %fusion.20 = f32[128,32,128]{2,0,1:T(8,128)S(1)} fusion(f32[128,32,128]{2,0,1:T(8,128)S(1)} %fusion.89, f32[128]{0:T(128)S(1)} %multiply_multiply_fusion.5, f32[128,32]{0,1:T(8,128)S(1)} %broadcast_add_fusion, f32[]{:T(128)S(6)} %convert_element_type.81, f32[128]{0:T(128)S(1)} %get-tuple-element.46, f32[128]{0:T(128)S(1)} %get-tuple-element.47, ...), kind=kOutput, calls=%fused_computation.32 | convolution fusion | flops 807485440 | bytes 4212868 | tf_op jit(solution)/shard_map/kx,klm->xlm/dot_general | solution.py:130
  282.7 1.2 copy.191
  283.9 26.3 %all_to_all.110 = f32[128,32,128]{2,1,0:T(8,128)S(1)} all-to-all(f32[128,32,128]{2,1,0:T(8,128)S(1)} %copy.191), channel_id=1, replica_groups=mesh['grp'=64,'sub'=4] {'sub'}, dimensions={0} | all-to-all | bytes 4194304 | tf_op jit(solution)/shard_map/all_to_all | solution.py:133
  311.0 3.6 fusion.68
  314.7 4.2 %fusion.17 = f32[32,128,128]{2,1,0:T(8,128)S(1)} fusion(f32[1,32,128,128]{3,2,1,0:T(8,128)S(1)} %copy-done.3, f32[32,128,128]{2,1,0:T(8,128)S(1)} %fusion.68, f32[32,128]{1,0:T(8,128)S(1)} %and_convert_fusion.1, f32[128]{0:T(128)S(1)} %get-tuple-element.45, f32[128]{0:T(128)S(1)} %get-tuple-element.46, f32[128]{0:T(128)S(1)} %get-tuple-element.47, ...), kind=kOutput, calls=%fused_computation.29 | convolution fusion | flops 806436864 | bytes 6309504 | tf_op jit(solution)/shard_map/mz,xym->xyz/dot_general | solution.py:46
  318.9 31.6 %all-gather.7.cloned.1.call-done = f32[512,3,1024]{2,0,1:T(8,128)} async-done(((f32[8,3,1024]{2,0,1:T(8,128)}), f32[512,3,1024]{2,0,1:T(8,128)}) %all-gather.7.cloned.1.call-update) | async-done | bytes 6291472 | tf_op jit(solution)/shard_map/all_gather | solution.py:143
  350.5 10.5 %copy.203 = f32[512,3,1024]{2,1,0:T(4,128)} copy(f32[512,3,1024]{2,0,1:T(8,128)} %all-gather.7.cloned.1.call-done) | data formatting | bytes 12582912 | tf_op jit(solution)/shard_map/all_gather | solution.py:143
  361.0 4.0 %gather_fusion.3 = f32[8,3,1024]{2,1,0:T(4,128)S(1)} fusion(f32[512,3,1024]{2,1,0:T(4,128)} %copy.203, s32[1024]{0:T(1024)S(1)} %pad_clamp_fusion), kind=kCustom, calls=%fused_computation.3 | custom fusion | bytes 196640 | tf_op jit(solution)/shard_map/gather | solution.py:145
  367.2 1.3 copy-done.4
  (105 shorter events, 11.1 us)
Async XLA Ops:
  20.9 30.0 %all-to-all-start = ((f32[32,128,128]{2,0,1:T(8,128)}), f32[32,128,128]{2,0,1:T(8,128)S(1)}, u32[]{:S(2)}, u32[]{:S(2)}) async-start(f32[32,128,128]{2,0,1:T(8,128)} %copy.159), calls=%async_computation | async-start | bytes 4194304 | tf_op jit(solution)/shard_map/all_to_all | solution.py:128
  61.3 29.1 %all-to-all-start.2 = ((f32[128,32,128]{2,1,0:T(8,128)}), f32[128,32,128]{2,1,0:T(8,128)}, u32[]{:S(2)}, u32[]{:S(2)}) async-start(f32[128,32,128]{2,1,0:T(8,128)} %copy.169), calls=%async_computation.2 | async-start | bytes 4194304 | tf_op jit(solution)/shard_map/all_to_all | solution.py:134
  65.7 112.5 %all-gather.5.cloned.1.call-start = ((), (), s32[]{:S(2)}) async-start(), calls=%async_computation.6 | async-start | bytes 6389760 | tf_op jit(solution)/shard_map/all_gather | solution.py:143
  107.7 3.8 %copy-start.6 = (s32[64,2,4]{0,2,1:T(4,128)S(1)}, s32[64,2,4]{0,2,1:T(4,128)}, u32[]{:S(2)}) copy-start(s32[64,2,4]{0,2,1:T(4,128)} %param.15) | copy-start | bytes 6148
  107.7 4.6 %copy-start = (s32[64]{0:T(128)S(1)}, s32[64]{0:T(128)}, u32[]{:S(2)}) copy-start(s32[64]{0:T(128)} %param.14) | copy-start | bytes 772
  107.7 5.2 %copy-start.1 = (s32[64,2]{0,1:T(2,128)S(1)}, s32[64,2]{0,1:T(2,128)}, u32[]{:S(2)}) copy-start(s32[64,2]{0,1:T(2,128)} %param.13) | copy-start | bytes 1540
  107.7 27.5 %all-to-all-start.1 = ((f32[128,32,128]{2,1,0:T(8,128)}), f32[128,32,128]{2,1,0:T(8,128)S(1)}, u32[]{:S(2)}, u32[]{:S(2)}) async-start(f32[128,32,128]{2,1,0:T(8,128)} %copy.163), calls=%async_computation.1 | async-start | bytes 4194304 | tf_op jit(solution)/shard_map/all_to_all | solution.py:133
  111.5 239.0 %all-gather.7.cloned.1.call-start = ((), (), s32[]{:S(2)}) async-start(), calls=%async_computation.7 | async-start | bytes 6389760 | tf_op jit(solution)/shard_map/all_gather | solution.py:143
  135.2 0.7 copy-start.10
  135.2 0.9 copy-start.9
  136.5 3.6 copy-start.5
  144.3 48.7 %copy-start.8 = (f32[3,3,1]{1,0,2:T(4,128)S(1)}, f32[3,3,1]{1,0,2:T(4,128)}, u32[]{:S(2)}) copy-start(f32[3,3,1]{1,0,2:T(4,128)} %constant.231) | copy-start | bytes 112
  144.3 48.9 %copy-start.7 = (f32[3,3,1]{1,0,2:T(4,128)S(1)}, f32[3,3,1]{1,0,2:T(4,128)}, u32[]{:S(2)}) copy-start(f32[3,3,1]{1,0,2:T(4,128)} %constant.228) | copy-start | bytes 112
  195.1 2.4 copy-start.2
  311.0 3.6 copy-start.3
  367.1 1.3 copy-start.4
Sparse Core Ops, SparseCore 0:
  95.4 82.8 all-gather.4
  272.7 77.7 all-gather.6
where the time goes:
time: 382 us; the launch traced here: 375 us
  waiting for transfers between devices  133 us (35%)
  blocking collectives  83.3 us (22%)
  matrix products  67.9 us (18%)
  local copies, waits for them, and re-layouts  52.8 us (14%)
  between operations  19.5 us (5%)
  starting transfers between devices  13 us (3%)
  other arithmetic  6.24 us (2%)
    all_gather x2, waiting for transfers between devices, reverse_step(): everyone = lax.all_gather(own_strips[None], 'grp', axis=0, tiled=True)  65.5 us
    all_to_all x1, blocking collectives, reverse_step(): lax.all_to_all(spectral, 'sub', split_axis=1, concat_axis=0, tiled=True)  29.8 us
    all_to_all x1, blocking collectives, reverse_step(): lax.all_to_all(force_part, 'sub', split_axis=0, concat_axis=1, tiled=True)  27.2 us
    all_to_all x1, blocking collectives, reverse_step(): lax.all_to_all(wave_part, 'sub', split_axis=0, concat_axis=1, tiled=True)  26.3 us
    all_to_all x1, waiting for transfers between devices, reverse_step(): lax.all_to_all(spectral, 'sub', split_axis=1, concat_axis=0, tiled=True)  24.2 us
    all_to_all x1, waiting for transfers between devices, reverse_step(): lax.all_to_all(force_part, 'sub', split_axis=0, concat_axis=1, tiled=True)  22.8 us
    all_gather x2, local copies, waits for them, and re-layouts, reverse_step(): everyone = lax.all_gather(own_strips[None], 'grp', axis=0, tiled=True)  21.2 us
    all_to_all x1, waiting for transfers between devices, reverse_step(): lax.all_to_all(wave_part, 'sub', split_axis=0, concat_axis=1, tiled=True)  20.2 us
  transfers between devices with their start and end apart: 5, of which 5 were waited for; matrix products, arithmetic and copies ran while one was open for 12% of the time, Pallas kernels for 0%

commit v1 on v0

v1 whole, which is shorter than its diff:
```python
import functools

import jax
import jax.numpy as jnp
from jax import lax
from jax.experimental import pallas as pl
from jax.experimental.pallas import tpu as pltpu
from jax.sharding import Mesh
from jax.sharding import PartitionSpec as P

time_step = 0.5
stencil_rows = (
    (0, 0, -2, 2, 0, 0),
    (0, 2, -27, 27, -2, 0),
    (-2, 27, -270, 270, -27, 2),
    (2, -27, 270, -270, 27, -2),
    (0, -2, 27, -27, 2, 0),
    (0, 0, 2, -2, 0, 0),
)
weights = [[stencil_rows[j][i] / 180.0 for j in range(6)] for i in range(6)]
sinc_terms = (1.0, -1.0 / 6, 1.0 / 120, -1.0 / 5040, 1.0 / 362880, -1.0 / 39916800, 1.0 / 6227020800)
MESH = pl.DeviceIdType.MESH
N = 128
X = 32
CHUNKS = 4
CX = X // CHUNKS
ROWS, RING, CORES, SUBS = 4, 8, 2, 4
f32 = jnp.float32
bf16 = jnp.bfloat16


def cosine_table(size_cells, length):
    mode_index = jnp.arange(size_cells, dtype=jnp.int32)[:, None]
    cell_index = jnp.arange(size_cells, dtype=jnp.int32)[None, :]
    extent = length.astype(jnp.float32)
    angles = (
        jnp.pi * mode_index.astype(jnp.float32) * (cell_index.astype(jnp.float32) + 0.5) / extent
    )
    scaling = jnp.sqrt(jnp.where(mode_index == 0, 1.0, 2.0).astype(jnp.float32) / extent)
    inside = (mode_index < length) & (cell_index < length)
    return jnp.where(inside, scaling * jnp.cos(angles), jnp.float32(0.0))


def parts_of(value):
    high = value.astype(bf16)
    return high, (value - high.astype(f32)).astype(bf16)


def left_stack(table):
    high, low = parts_of(table)
    return jnp.concatenate(
        [jnp.concatenate([high, high], 1), jnp.concatenate([low, jnp.zeros_like(low)], 1)], 0
    )


def right_stack(table):
    high, low = parts_of(table)
    return jnp.concatenate(
        [jnp.concatenate([high, low], 1), jnp.concatenate([high, jnp.zeros_like(low)], 1)], 0
    )


def times_right(value, stack):
    high, low = parts_of(value)
    out = jnp.dot(jnp.concatenate([high, low], 1), stack, preferred_element_type=f32)
    return out[:, :N] + out[:, N:]


def left_times(stack, pair):
    high, low = parts_of(pair)
    out = jnp.dot(stack, jnp.concatenate([high, low], 0), preferred_element_type=f32)
    return out[:N] + out[N:]


def kernel(
    ints, floats, adj_next, adj_later, tables, base, limits,
    out_now, out_earlier,
    fields, stage, recv, back, land, stacks, modes, wave, source,
    faces, face_send, face_in, near_first, near_second, wanted, wanted_in, coup, coup_send, coup_all, coup_modes,
    load_sem, store_sem, local_sem, big_send, big_recv,
    face_ssem, face_rsem, ring_ssem, ring_rsem, core_ssem, core_rsem,
    row_ssem, row_rsem, all_ssem, all_rsem,
):
    row, ring = lax.axis_index("row"), lax.axis_index("z")
    core, sub = lax.axis_index("core"), lax.axis_index("sub")
    inputs = (adj_next, adj_later)
    outputs = (out_now, out_earlier)
    recv_flat = [recv.at[i].reshape(N * X, N) for i in range(2)]
    back_flat = [back.at[i].reshape(N * X, N) for i in range(2)]
    near = (near_first, near_second)
    sent = []

    def load(i, c):
        return pltpu.make_async_copy(
            inputs[i].at[0, pl.ds(CX * c, CX)], fields.at[i, pl.ds(CX * c, CX)], load_sem.at[i, c]
        )

    for i in range(2):
        for c in range(CHUNKS):
            load(i, c).start()

    barrier = pltpu.get_barrier_semaphore()
    for j in (1, 2, 3):
        pl.semaphore_signal(barrier, inc=1, device_id={"sub": lax.rem(sub + j, SUBS)}, device_id_type=MESH)
        pl.semaphore_signal(barrier, inc=1, device_id={"row": lax.rem(row + j, ROWS)}, device_id_type=MESH)
    for j in (1, RING - 1):
        pl.semaphore_signal(barrier, inc=1, device_id={"z": lax.rem(ring + j, RING)}, device_id_type=MESH)
    pl.semaphore_signal(barrier, inc=1, device_id={"core": 1 - core}, device_id_type=MESH)

    for i in range(4):
        stacks[i] = left_stack(tables[i])
    for i in (4, 5):
        stacks[i] = right_stack(tables[i])
    pl.semaphore_wait(barrier, 9)

    def remote(src, dst, ssem, rsem, where):
        copy = pltpu.make_async_remote_copy(
            src_ref=src, dst_ref=dst, send_sem=ssem, recv_sem=rsem, device_id=where, device_id_type=MESH
        )
        return copy

    def post(copy):
        copy.start()
        sent.append(copy)

    def large(a, c, j):
        d = lax.rem(sub + j, SUBS)
        if a < 2:
            src = stage.at[a, pl.ds(CX * c, CX), pl.ds(X * d, X), :]
            dst = recv.at[a, pl.ds(X * sub + CX * c, CX)]
        else:
            src = back.at[a - 2, pl.ds(X * d + CX * c, CX)]
            dst = land.at[a - 2, pl.ds(CX * c, CX), pl.ds(X * sub, X), :]
        return src, dst, d

    def large_copy(a, c, j):
        src, dst, d = large(a, c, j)
        if j == 0:
            return pltpu.make_async_copy(src, dst, local_sem.at[a, c])
        return remote(src, dst, big_send.at[a, c, j - 1], big_recv.at[a, c, j - 1], {"sub": d})

    def large_start(a, c):
        for j in (2, 1, 3):
            post(large_copy(a, c, j))
        large_copy(a, c, 0).start()

    def large_wait(a, c):
        large_copy(a, c, 0).wait()
        for j in (1, 3, 2):
            large_copy(a, c, j).wait_recv()

    def forward_chunk(i, c):
        def step(p, carry):
            x0 = CX * c + 2 * p
            value = times_right(fields[i, pl.ds(x0, 2)].reshape(2 * N, N), stacks[4])
            value = left_times(stacks[2], jnp.concatenate([value[:N], value[N:]], 1))
            stage[i, x0] = value[:, :N]
            stage[i, x0 + 1] = value[:, N:]
            return carry

        lax.fori_loop(0, CX // 2, step, 0, unroll=2)

    def to_modes(i, l0):
        pair = jnp.concatenate(
            [
                recv_flat[i][pl.ds(l0, N, stride=X), :],
                recv_flat[i][pl.ds(l0 + 1, N, stride=X), :],
            ],
            1,
        )
        return left_times(stacks[0], pair)

    def from_modes(i, l0, pair):
        value = left_times(stacks[1], pair)
        back_flat[i][pl.ds(l0, N, stride=X), :] = value[:, :N]
        back_flat[i][pl.ds(l0 + 1, N, stride=X), :] = value[:, N:]

    def add_faces(l0, first, second):
        for r in range(6):
            faces[r] = faces[r] + (floats[X + 6 * l0 + r] * first + floats[X + 6 * l0 + 6 + r] * second)

    def face_copy(e, j):
        d = lax.rem(sub + j, SUBS)
        return remote(
            face_send.at[e, :, pl.ds(X * d, X), :],
            face_in.at[e, j - 1],
            face_ssem.at[e, j - 1],
            face_rsem.at[e, j - 1],
            {"sub": d},
        )

    def faces_start(e):
        for r in (0, 2, 4):
            value = left_times(stacks[1], jnp.concatenate([faces[r], faces[r + 1]], 1))
            face_send[e, r] = value[:, :N]
            face_send[e, r + 1] = value[:, N:]
        for j in (2, 1, 3):
            post(face_copy(e, j))

    def slot(k):
        return lax.rem(ring + k + RING, RING) * CORES + core

    def ring_copy(e, h, side):
        owner = -(h - 1) if side == 0 else h - 1
        k = h - 1 if side == 0 else 3 + h
        block = near[e].at[slot(owner)]
        target = lax.rem(ring + (1 if side == 0 else RING - 1), RING)
        return remote(block, block, ring_ssem.at[e, k], ring_rsem.at[e, k], {"z": target})

    def core_copy(e, k):
        owner = -k if k < 5 else k - 4
        block = near[e].at[slot(owner)]
        return remote(block, block, core_ssem.at[e, k], core_rsem.at[e, k], {"core": 1 - core})

    def row_copy(e, j):
        return remote(
            wanted.at[e, j],
            wanted_in.at[e, j - 1],
            row_ssem.at[e, j - 1],
            row_rsem.at[e, j - 1],
            {"row": lax.rem(row + j, ROWS)},
        )

    def exchange(e, fill):
        fill = list(fill)

        def other_work():
            if fill:
                fill.pop(0)()

        other_work()
        for j in (1, 3, 2):
            face_copy(e, j).wait_recv()
        own = face_send[e, :, pl.ds(X * sub, X), :] + face_in[e, 0] + face_in[e, 1] + face_in[e, 2]
        own = times_right(own.reshape(6 * X, N), stacks[5]).reshape(6, X, N)
        near[e][slot(0)] = own
        post(ring_copy(e, 1, 0))
        post(ring_copy(e, 1, 1))
        post(core_copy(e, 0))
        for h in (1, 2, 3, 4):
            other_work()
            ring_copy(e, h, 0).wait_recv()
            if h < 4:
                post(ring_copy(e, h + 1, 0))
            post(core_copy(e, h))
            if h < 4:
                ring_copy(e, h, 1).wait_recv()
                if h < 3:
                    post(ring_copy(e, h + 1, 1))
                post(core_copy(e, 4 + h))
        other_work()
        for k in range(8):
            core_copy(e, k).wait_recv()

        lane = lax.broadcasted_iota(jnp.int32, (3, X, N), 2) // (N // 4)

        def choose(j, carry):
            for face in range(2):
                total = jnp.zeros((3, X, N), f32)
                for seg in range(4):
                    at = 2 + 3 * (8 * j + 4 * face + seg)
                    value = near[e][ints[at], 3 * (1 - face) : 3 * (1 - face) + 3]
                    shift = jnp.full((3, X, N), ints[at + 1], jnp.int32)
                    value = jnp.where(shift % 2 == 1, pltpu.roll(value, N // 4, 2), value)
                    value = jnp.where(shift >= 2, pltpu.roll(value, N // 2, 2), value)
                    taken = (lane == seg) & (jnp.full((3, X, N), ints[at + 2], jnp.int32) == 1)
                    total = jnp.where(taken, value, total)
                wanted[e, j, 3 * face : 3 * face + 3] = total
            return carry

        lax.fori_loop(0, ROWS, choose, 0)
        for j in (2, 1, 3):
            post(row_copy(e, j))
        for work in fill:
            work()
        for j in (1, 3, 2):
            row_copy(e, j).wait_recv()
        other = wanted[e, 0] + wanted_in[e, 0] + wanted_in[e, 1] + wanted_in[e, 2]
        own = near[e][slot(0)]
        x_here = (sub * X + lax.broadcasted_iota(jnp.int32, (X, N), 0)).astype(f32)
        for face in range(2):
            limit = jnp.broadcast_to(limits[pl.ds(face, 1), :], (X, N))
            joined = x_here < limit
            values = [other[0], other[1], other[2], own[0], own[1], own[2]]
            if face == 1:
                values = [own[3], own[4], own[5], other[3], other[4], other[5]]
            for i in range(3):
                line = weights[3 * (1 - face) + i]
                term = sum(line[k] * values[k] for k in range(6) if line[k] != 0.0)
                coup[e, 3 * face + i] = jnp.where(joined, term, 0.0)

    len_x, len_y = ints[0], ints[1]
    y_index = lax.broadcasted_iota(jnp.int32, (N, N), 0)
    face_rows = [0, 1, 2, len_y - 3, len_y - 2, len_y - 1]

    def finish_chunk(i, c):
        def step(p, carry):
            x0 = CX * c + 2 * p
            value = left_times(stacks[3], jnp.concatenate([land[i, x0], land[i, x0 + 1]], 1))
            value = times_right(jnp.concatenate([value[:, :N], value[:, N:]], 0), stacks[5])
            for q in range(2):
                x = x0 + q
                result = value[N * q : N * q + N]
                inside = (y_index < len_y) & (jnp.full((N, N), sub * X + x, jnp.int32) < len_x)
                result = result - jnp.where(inside, fields[1 - i, x], 0.0)
                extra = jnp.zeros((N, N), f32)
                for r in range(6):
                    line = jnp.broadcast_to(coup[i, r, pl.ds(x, 1), :], (N, N))
                    extra = jnp.where(y_index == face_rows[r], line, extra)
                land[i, x] = result + extra
            return carry

        lax.fori_loop(0, CX // 2, step, 0, unroll=2)
        store(i, c).start()

    def store(i, c):
        return pltpu.make_async_copy(
            land.at[i, pl.ds(CX * c, CX)], outputs[i].at[0, pl.ds(CX * c, CX)], store_sem.at[i, c]
        )

    for c in range(CHUNKS):
        load(0, c).wait()
        forward_chunk(0, c)
        large_start(0, c)
    for c in range(CHUNKS):
        load(1, c).wait()
        forward_chunk(1, c)
        if c == 0:
            large_start(1, 0)

    def factors(l, carry):
        square = base[...] + floats[l]
        series = jnp.full((N, N), sinc_terms[-1], f32)
        for term in sinc_terms[-2::-1]:
            series = series * square + f32(term)
        unit = series * series
        wave[l] = 2.0 - 4.0 * (square * unit)
        source[l] = time_step**2 * unit
        return carry

    lax.fori_loop(0, X, factors, 0, unroll=2)
    for r in range(6):
        faces[r] = jnp.zeros((N, N), f32)
    for c in range(CHUNKS):
        large_wait(0, c)

    def first_modes(p, carry):
        l0 = 2 * p
        value = to_modes(0, l0)
        modes[0, l0] = value[:, :N]
        modes[0, l0 + 1] = value[:, N:]
        add_faces(l0, source[l0] * value[:, :N], source[l0 + 1] * value[:, N:])
        return carry

    lax.fori_loop(0, X // 2, first_modes, 0, unroll=2)
    faces_start(0)
    large_start(1, 1)

    def first_back(p, carry):
        l0 = 2 * p
        pair = jnp.concatenate([wave[l0] * modes[0, l0], wave[l0 + 1] * modes[0, l0 + 1]], 1)
        from_modes(0, l0, pair)
        return carry

    lax.fori_loop(0, X // 2, first_back, 0, unroll=2)

    def start(a, c):
        return lambda: large_start(a, c)

    def later_modes():
        for c in range(CHUNKS):
            large_wait(1, c)

        def step(p, carry):
            l0 = 2 * p
            value = to_modes(1, l0)
            modes[1, l0] = value[:, :N]
            modes[1, l0 + 1] = value[:, N:]
            return carry

        lax.fori_loop(0, X // 2, step, 0, unroll=2)

    exchange(
        0,
        [start(1, 2), start(1, 3), start(2, 0), start(2, 1), start(2, 2), start(2, 3), later_modes],
    )

    def all_copy(j):
        return remote(
            coup_send,
            coup_all.at[:, pl.ds(X * sub, X), :],
            all_ssem.at[j - 1],
            all_rsem.at[j - 1],
            {"sub": lax.rem(sub + j, SUBS)},
        )

    coup_rows = times_right(coup[0].reshape(6 * X, N), stacks[4]).reshape(6, X, N)
    coup_send[...] = coup_rows
    coup_all[:, pl.ds(X * sub, X), :] = coup_rows
    for j in (2, 1, 3):
        post(all_copy(j))
    for r in range(6):
        faces[r] = jnp.zeros((N, N), f32)
    for j in (1, 3, 2):
        all_copy(j).wait_recv()
    for r in (0, 2, 4):
        value = left_times(stacks[0], jnp.concatenate([coup_all[r], coup_all[r + 1]], 1))
        coup_modes[r] = value[:, :N]
        coup_modes[r + 1] = value[:, N:]

    def second_modes(p, carry):
        l0 = 2 * p
        pair = []
        for q in range(2):
            l = l0 + q
            value = wave[l] * modes[0, l] - modes[1, l]
            for r in range(6):
                value = value + floats[X + 6 * l + r] * coup_modes[r]
            modes[1, l] = value
            pair.append(value)
        add_faces(l0, source[l0] * pair[0], source[l0 + 1] * pair[1])
        return carry

    lax.fori_loop(0, X // 2, second_modes, 0)
    faces_start(1)

    def second_back(p, carry):
        l0 = 2 * p
        pair = jnp.concatenate([wave[l0] * modes[1, l0], wave[l0 + 1] * modes[1, l0 + 1]], 1)
        from_modes(1, l0, pair)
        return carry

    lax.fori_loop(0, X // 2, second_back, 0, unroll=2)
    for c in range(CHUNKS):
        large_start(3, c)

    def finish(i, c):
        def work():
            large_wait(2 + i, c)
            finish_chunk(i, c)

        return work

    exchange(1, [finish(0, 0), finish(0, 1), finish(0, 2), finish(0, 3)])
    for c in range(CHUNKS):
        finish(1, c)()
    for copy in sent:
        copy.wait_send()
    for i in range(2):
        for c in range(CHUNKS):
            store(i, c).wait()


def local(adj_next, adj_later, box_sizes, holder, partner):
    part_count = holder.shape[0]
    seg_count = partner.shape[2]
    item_count = 2 * seg_count
    plane = RING * CORES
    my_row = lax.axis_index("row")
    my_place = lax.axis_index("z") * CORES + lax.axis_index("core")
    my_column = lax.axis_index("sub")
    part_ids = jnp.arange(part_count, dtype=jnp.int32)
    row_ids = (my_row + jnp.arange(ROWS, dtype=jnp.int32)) % ROWS
    groups = row_ids * plane + my_place
    row_parts = jnp.sum(jnp.where(holder[None, :] == groups[:, None], part_ids[None, :], 0), axis=1)
    my_part = row_parts[0]
    len_x = box_sizes[my_part, 0]
    len_y = box_sizes[my_part, 1]
    table_x = cosine_table(N, len_x)
    table_y = cosine_table(N, len_y)
    table_z = cosine_table(N, jnp.int32(N))
    tables = jnp.stack([table_x, table_x.T, table_y, table_y.T, table_z.T, table_z])
    my_modes = lax.dynamic_slice_in_dim(table_y, my_column * X, X, 0)
    my_face = jnp.concatenate(
        [my_modes[:, 0:3], lax.dynamic_slice_in_dim(my_modes, len_y - 3, 3, 1)], axis=1
    )
    count = jnp.arange(N, dtype=jnp.int32).astype(f32)
    quarter = f32((jnp.pi * time_step / 2) ** 2)
    square_x = quarter * (count / len_x.astype(f32)) ** 2
    square_z = quarter * (count / f32(N)) ** 2
    mode_y = (my_column * X + jnp.arange(X, dtype=jnp.int32)).astype(f32)
    square_y = quarter * (mode_y / len_y.astype(f32)) ** 2
    base = square_x[:, None] + square_z[None, :]
    floats = jnp.concatenate([square_y, my_face.reshape(-1)])
    item_ids = jnp.arange(item_count, dtype=jnp.int32)
    link_ids = partner[row_parts].reshape(ROWS, item_count)
    safe_links = jnp.maximum(link_ids, 0)
    peer_part = safe_links // seg_count
    peer_seg = safe_links % seg_count
    peer_group = holder[peer_part]
    shift = (item_ids[None, :] % seg_count - peer_seg) % seg_count
    here = (peer_group // plane == my_row) & (link_ids >= 0)
    picks = jnp.stack([peer_group % plane, shift, here.astype(jnp.int32)], axis=-1)
    ints = jnp.concatenate([jnp.stack([len_x, len_y]), picks.reshape(-1)])
    x_limit = jnp.where(link_ids[0] >= 0, jnp.minimum(len_x, box_sizes[peer_part[0], 0]), 0)
    limits = jnp.repeat(x_limit.reshape(2, seg_count), N // seg_count, axis=1).astype(f32)
    limits = jnp.concatenate([limits, jnp.zeros((6, N), f32)], axis=0)

    vmem = pl.BlockSpec(memory_space=pltpu.VMEM)
    smem = pl.BlockSpec(memory_space=pltpu.SMEM)
    anywhere = pl.BlockSpec(memory_space=pl.ANY)
    block = jax.ShapeDtypeStruct((1, X, N, N), f32)
    dma = pltpu.SemaphoreType.DMA
    return pl.pallas_call(
        kernel,
        out_shape=(block, block),
        in_specs=[smem, smem, anywhere, anywhere, vmem, vmem, vmem],
        out_specs=(anywhere, anywhere),
        scratch_shapes=[
            pltpu.VMEM((2, X, N, N), f32),
            pltpu.VMEM((2, X, N, N), f32),
            pltpu.VMEM((2, N, X, N), f32),
            pltpu.VMEM((2, N, X, N), f32),
            pltpu.VMEM((2, X, N, N), f32),
            pltpu.VMEM((6, 2 * N, 2 * N), bf16),
            pltpu.VMEM((2, X, N, N), f32),
            pltpu.VMEM((X, N, N), f32),
            pltpu.VMEM((X, N, N), f32),
            pltpu.VMEM((6, N, N), f32),
            pltpu.VMEM((2, 6, N, N), f32),
            pltpu.VMEM((2, 3, 6, X, N), f32),
            pltpu.VMEM((plane, 6, X, N), f32),
            pltpu.VMEM((plane, 6, X, N), f32),
            pltpu.VMEM((2, ROWS, 6, X, N), f32),
            pltpu.VMEM((2, 3, 6, X, N), f32),
            pltpu.VMEM((2, 6, X, N), f32),
            pltpu.VMEM((6, X, N), f32),
            pltpu.VMEM((6, N, N), f32),
            pltpu.VMEM((6, N, N), f32),
            dma((2, CHUNKS)),
            dma((2, CHUNKS)),
            dma((4, CHUNKS)),
            dma((4, CHUNKS, 3)),
            dma((4, CHUNKS, 3)),
            dma((2, 3)),
            dma((2, 3)),
            dma((2, 7)),
            dma((2, 7)),
            dma((2, 8)),
            dma((2, 8)),
            dma((2, 3)),
            dma((2, 3)),
            dma((3,)),
            dma((3,)),
        ],
        compiler_params=pltpu.CompilerParams(
            collective_id=0, has_side_effects=True, vmem_limit_bytes=64 * 1000 * 1000
        ),
        name="two_steps",
    )(ints, floats, adj_next, adj_later, tables, base, limits)


def solution(mesh):
    devices = mesh.devices
    split = Mesh(devices.reshape(ROWS, RING, CORES, SUBS), ("row", "z", "core", "sub"))
    field = P(("row", "z", "core"), "sub", None, None)
    return jax.shard_map(
        local,
        mesh=split,
        in_specs=(field, field, P(), P(), P()),
        out_specs=(field, field),
        check_vma=False,
    )
```

time: 382 us -> 156 us (0.41); the launches traced: 375 us -> 154 us
  waiting for transfers between devices: 133 us -> 0 us
  Pallas kernels: 0 us -> 129 us
  blocking collectives: 83.3 us -> 0 us
  matrix products: 67.9 us -> 0 us
  local copies, waits for them, and re-layouts: 52.8 us -> 12.5 us
  between operations: 19.5 us -> 3.71 us
  starting transfers between devices: 13 us -> 0 us
    pallas_call x0 -> x1, Pallas kernels: none -> 129 us  [local(): pl.pallas_call(kernel, out_shape=(block, block), in_specs=[smem, smem, an...]
    all_to_all x3 -> x0, blocking collectives: 83.3 us -> none  [the longest x1 29.8 us: reverse_step(): lax.all_to_all(spectral, 'sub', split_axis=1, concat_axis=0, tiled=True)]
    dot_general x26 -> x0, matrix products: 67.9 us -> none  [the longest x2 20 us: reverse_step(): jnp.einsum('kx,klm->xlm', table_x, two_cos * spectral, precision=precise)]
    all_to_all x3 -> x0, waiting for transfers between devices: 67.2 us -> none  [the longest x1 24.2 us: reverse_step(): lax.all_to_all(spectral, 'sub', split_axis=1, concat_axis=0, tiled=True)]
    all_gather x2 -> x0, waiting for transfers between devices: 65.5 us -> none  [reverse_step(): everyone = lax.all_gather(own_strips[None], 'grp', axis=0, tiled=True)]
    all_gather x2 -> x0, local copies, waits for them, and re-layouts: 21.2 us -> none  [reverse_step(): everyone = lax.all_gather(own_strips[None], 'grp', axis=0, tiled=True)]
    all_to_all x3 -> x0, starting transfers between devices: 12.7 us -> none  [the longest x1 4.54 us: reverse_step(): lax.all_to_all(spectral, 'sub', split_axis=1, concat_axis=0, tiled=True)]
    dot_general x4 -> x0, local copies, waits for them, and re-layouts: 7.51 us -> none  [the longest x2 3.75 us: reverse_step(): jnp.einsum('kx,klm->xlm', table_x, source * spectral, precision=precise)]
  transfers between devices with their start and end apart: 5 -> 0, of which waited for: 5 -> 0; matrix products, arithmetic and copies ran while one was open for 12% -> 0% of each run, Pallas kernels for 0% -> 0%
where the time goes in v1:
time: 156 us; the launch traced here: 154 us
  Pallas kernels  129 us (83%)
  local copies, waits for them, and re-layouts  12.5 us (8%)
  other arithmetic  8.5 us (5%)
  between operations  3.71 us (2%)
    pallas_call x1, Pallas kernels, local(): pl.pallas_call(kernel, out_shape=(block, block), in_specs=[smem, smem, an...  129 us
    unnamed x9, local copies, waits for them, and re-layouts  6.15 us

profile of v1, /device:TPU:9, one launch (start us, length us, event | category | flops | bytes accessed | tf_op | source)
XLA Modules:
  0.0 153.7 jit_solution(3339484373617313899)
XLA Ops:
  0.6 0.0 copy-start
  0.7 0.9 select_reduce_fusion
  1.7 1.4 constant_dynamic-slice_fusion.1
  5.9 0.7 iota_compare_fusion.2
  6.6 0.7 iota_compare_fusion.1
  7.3 0.7 broadcast_add_fusion.base
  8.0 0.3 multiply_select_fusion
  8.3 0.1 constant_dynamic-slice_fusion
  8.4 0.1 copy.76
  8.5 0.1 reshape.1086
  8.6 0.6 pad_maximum_fusion.1.floats
  9.2 0.8 copy.61
  10.0 0.6 gather_fusion
  10.6 0.1 copy.77
  10.7 0.1 copy.62
  10.8 0.1 copy.74
  11.0 0.1 copy.80
  11.1 0.1 copy.81
  11.2 0.1 add_select_fusion.2
  11.2 0.1 copy.66
  11.3 0.1 reshape.1097
  11.4 0.1 slice_reduce_fusion
  11.5 1.3 gather_fusion.2
  12.9 0.7 broadcast_minimum_fusion
  13.5 0.1 min.12
  13.6 0.1 broadcast_in_dim.59
  13.7 0.1 convert_element_type.75
  13.8 0.6 concatenate.19.limits
  14.4 0.0 copy-done
  14.4 0.7 gather_fusion.1
  15.1 0.1 gather.13
  15.2 0.1 copy.67
  15.3 0.1 copy.75
  15.5 0.1 reshape.1085
  15.6 1.9 %pad_add_fusion.1.ints = s32[98]{0:T(128)} fusion(s32[96]{0:T(128)S(1)} %reshape.1085, s32[1]{0:T(128)} %bitcast.2, s32[1]{0:T(128)} %bitcast.1), kind=kLoop, calls=%fused_computation.87 | loop fusion | flops 196 | bytes 784 | tf_op jit(solution)/shard_map/concatenate | solution.py:494
  17.5 0.3 fusion.2
  17.8 0.3 fusion.8
  18.1 0.3 fusion.5
  18.4 0.3 fusion.11
  18.7 0.3 fusion.12
  19.0 0.3 fusion.13.tables
  19.4 0.0 copy-start.2
  19.4 0.7 copy-done.2
  20.1 129.0 %two_steps.1 = (f32[1,32,128,128]{3,2,1,0:T(8,128)}, f32[1,32,128,128]{3,2,1,0:T(8,128)}) custom-call(s32[98]{0:T(128)} %pad_add_fusion.1.ints, f32[224]{0:T(256)} %pad_maximum_fusion.1.floats, f32[1,32,128,128]{3,2,1,0:T(8,128)} %adj_next.1, f32[1,32,128,128]{3,2,1,0:T(8,128)} %adj_later.1, f32[6,128,128]{2,1,0:T(8,128)} %copy-done.2, ...), custom_call_target="tpu_custom_call" | custom-call | tf_op jit(solution)/shard_map/two_steps/pallas_call | solution.py:504
  149.1 0.0 copy-start.1
  149.1 3.3 %copy.90 = f32[1,32,128,128]{3,2,1,0:T(8,128)} copy(f32[1,32,128,128]{3,2,1,0:T(8,128)} %get-tuple-element.21) | data formatting | bytes 4194304
  152.4 0.0 copy-done.1
  152.4 1.3 copy.91
  (20 shorter events, 0.2 us)
Async XLA Ops:
  0.6 13.8 %copy-start = (s32[64]{0:T(128)S(1)}, s32[64]{0:T(128)}, u32[]{:S(2)}) copy-start(s32[64]{0:T(128)} %param.8) | copy-start | bytes 772
  19.4 0.7 copy-start.2
  149.1 3.3 %copy-start.1 = (f32[1,32,128,128]{3,2,1,0:T(8,128)S(1)}, f32[1,32,128,128]{3,2,1,0:T(8,128)}, u32[]{:S(2)}) copy-start(f32[1,32,128,128]{3,2,1,0:T(8,128)} %get-tuple-element.22) | copy-start | bytes 6291460

commit v2 on v1

--- a/solution.py
+++ b/solution.py
@@ -29,16 +29,23 @@
 bf16 = jnp.bfloat16
 
 
-def cosine_table(size_cells, length):
-    mode_index = jnp.arange(size_cells, dtype=jnp.int32)[:, None]
-    cell_index = jnp.arange(size_cells, dtype=jnp.int32)[None, :]
-    extent = length.astype(jnp.float32)
-    angles = (
-        jnp.pi * mode_index.astype(jnp.float32) * (cell_index.astype(jnp.float32) + 0.5) / extent
-    )
-    scaling = jnp.sqrt(jnp.where(mode_index == 0, 1.0, 2.0).astype(jnp.float32) / extent)
-    inside = (mode_index < length) & (cell_index < length)
-    return jnp.where(inside, scaling * jnp.cos(angles), jnp.float32(0.0))
+def sinc_series(square):
+    series = jnp.full_like(square, sinc_terms[-1])
+    for term in sinc_terms[-2::-1]:
+        series = series * square + f32(term)
+    return series
+
+
+def cosine(mode, cell, length):
+    extent = jnp.full(mode.shape, length, jnp.int32).astype(f32)
+    period = 4.0 * extent
+    steps = (mode * (2 * cell + 1)).astype(f32)
+    steps = steps - period * jnp.floor(steps / period) - 2.0 * extent
+    half = steps * (f32(jnp.pi) / period)
+    sine = half * sinc_series(half * half)
+    scaling = jnp.sqrt(jnp.where(mode == 0, 1.0, 2.0) / extent)
+    value = scaling * (2.0 * (sine * sine) - 1.0)
+    return jnp.where((mode < length) & (cell < length), value, 0.0)
 
 
 def parts_of(value):
@@ -73,9 +80,9 @@
 
 
 def kernel(
-    ints, floats, adj_next, adj_later, tables, base, limits,
+    picks, limits, adj_next, adj_later,
     out_now, out_earlier,
-    fields, stage, recv, back, land, stacks, modes, wave, source,
+    fields, stage, recv, back, land, stacks, base, by_mode, modes, wave, source,
     faces, face_send, face_in, near_first, near_second, wanted, wanted_in, coup, coup_send, coup_all, coup_modes,
     load_sem, store_sem, local_sem, big_send, big_recv,
     face_ssem, face_rsem, ring_ssem, ring_rsem, core_ssem, core_rsem,
@@ -107,10 +114,34 @@
         pl.semaphore_signal(barrier, inc=1, device_id={"z": lax.rem(ring + j, RING)}, device_id_type=MESH)
     pl.semaphore_signal(barrier, inc=1, device_id={"core": 1 - core}, device_id_type=MESH)
 
-    for i in range(4):
-        stacks[i] = left_stack(tables[i])
-    for i in (4, 5):
-        stacks[i] = right_stack(tables[i])
+    place = ring * CORES + core
+    plane = RING * CORES
+
+    len_x, len_y = picks[96], picks[97]
+    down = lax.broadcasted_iota(jnp.int32, (N, N), 0)
+    across = lax.broadcasted_iota(jnp.int32, (N, N), 1)
+    stacks[2] = left_stack(cosine(down, across, len_y))
+    stacks[4] = right_stack(cosine(across, down, N))
+
+    def other_tables():
+        stacks[0] = left_stack(cosine(down, across, len_x))
+        stacks[1] = left_stack(cosine(across, down, len_x))
+        stacks[3] = left_stack(cosine(across, down, len_y))
+        stacks[5] = right_stack(cosine(down, across, N))
+        quarter = f32((jnp.pi * time_step / 2) ** 2)
+        ratio_x = down.astype(f32) / jnp.full((N, N), len_x, jnp.int32).astype(f32)
+        ratio_z = across.astype(f32) / f32(N)
+        base[...] = quarter * (ratio_x * ratio_x + ratio_z * ratio_z)
+        index = lax.broadcasted_iota(jnp.int32, (8 * X, N), 0)
+        mode, kind = sub * X + (index >> 3), index & 7
+        cell = jnp.where(kind < 3, kind, len_y - 6 + kind)
+        ratio_y = mode.astype(f32) / jnp.full((8 * X, N), len_y, jnp.int32).astype(f32)
+        by_mode[...] = jnp.where(kind < 6, cosine(mode, cell, len_y), quarter * (ratio_y * ratio_y))
+
+    other_tables()
+    def per_mode(l, kind):
+        return jnp.broadcast_to(by_mode[pl.ds(8 * l + kind, 1), :], (N, N))
+
     pl.semaphore_wait(barrier, 9)
 
     def remote(src, dst, ssem, rsem, where):
@@ -177,7 +208,7 @@
 
     def add_faces(l0, first, second):
         for r in range(6):
-            faces[r] = faces[r] + (floats[X + 6 * l0 + r] * first + floats[X + 6 * l0 + 6 + r] * second)
+            faces[r] = faces[r] + (per_mode(l0, r) * first + per_mode(l0 + 1, r) * second)
 
     def face_copy(e, j):
         d = lax.rem(sub + j, SUBS)
@@ -258,12 +289,12 @@
             for face in range(2):
                 total = jnp.zeros((3, X, N), f32)
                 for seg in range(4):
-                    at = 2 + 3 * (8 * j + 4 * face + seg)
-                    value = near[e][ints[at], 3 * (1 - face) : 3 * (1 - face) + 3]
-                    shift = jnp.full((3, X, N), ints[at + 1], jnp.int32)
-                    value = jnp.where(shift % 2 == 1, pltpu.roll(value, N // 4, 2), value)
+                    at = 3 * (8 * j + 4 * face + seg)
+                    value = near[e][picks[at], 3 * (1 - face) : 3 * (1 - face) + 3]
+                    shift = jnp.full((3, X, N), picks[at + 1], jnp.int32)
+                    value = jnp.where((shift & 1) == 1, pltpu.roll(value, N // 4, 2), value)
                     value = jnp.where(shift >= 2, pltpu.roll(value, N // 2, 2), value)
-                    taken = (lane == seg) & (jnp.full((3, X, N), ints[at + 2], jnp.int32) == 1)
+                    taken = (lane == seg) & (jnp.full((3, X, N), picks[at + 2], jnp.int32) == 1)
                     total = jnp.where(taken, value, total)
                 wanted[e, j, 3 * face : 3 * face + 3] = total
             return carry
@@ -277,10 +308,9 @@
             row_copy(e, j).wait_recv()
         other = wanted[e, 0] + wanted_in[e, 0] + wanted_in[e, 1] + wanted_in[e, 2]
         own = near[e][slot(0)]
-        x_here = (sub * X + lax.broadcasted_iota(jnp.int32, (X, N), 0)).astype(f32)
+        x_here = sub * X + lax.broadcasted_iota(jnp.int32, (X, N), 0)
         for face in range(2):
-            limit = jnp.broadcast_to(limits[pl.ds(face, 1), :], (X, N))
-            joined = x_here < limit
+            joined = x_here < jnp.broadcast_to(limits[pl.ds(face, 1), :], (X, N))
             values = [other[0], other[1], other[2], own[0], own[1], own[2]]
             if face == 1:
                 values = [own[3], own[4], own[5], other[3], other[4], other[5]]
@@ -289,8 +319,7 @@
                 term = sum(line[k] * values[k] for k in range(6) if line[k] != 0.0)
                 coup[e, 3 * face + i] = jnp.where(joined, term, 0.0)
 
-    len_x, len_y = ints[0], ints[1]
-    y_index = lax.broadcasted_iota(jnp.int32, (N, N), 0)
+    y_index = down
     face_rows = [0, 1, 2, len_y - 3, len_y - 2, len_y - 1]
 
     def finish_chunk(i, c):
@@ -329,11 +358,9 @@
             large_start(1, 0)
 
     def factors(l, carry):
-        square = base[...] + floats[l]
-        series = jnp.full((N, N), sinc_terms[-1], f32)
-        for term in sinc_terms[-2::-1]:
-            series = series * square + f32(term)
-        unit = series * series
+        square = base[...] + per_mode(l, 6)
+        unit = sinc_series(square)
+        unit = unit * unit
         wave[l] = 2.0 - 4.0 * (square * unit)
         source[l] = time_step**2 * unit
         return carry
@@ -415,7 +442,7 @@
             l = l0 + q
             value = wave[l] * modes[0, l] - modes[1, l]
             for r in range(6):
-                value = value + floats[X + 6 * l + r] * coup_modes[r]
+                value = value + per_mode(l, r) * coup_modes[r]
             modes[1, l] = value
             pair.append(value)
         add_faces(l0, source[l0] * pair[0], source[l0 + 1] * pair[1])
@@ -458,7 +485,6 @@
     plane = RING * CORES
     my_row = lax.axis_index("row")
     my_place = lax.axis_index("z") * CORES + lax.axis_index("core")
-    my_column = lax.axis_index("sub")
     part_ids = jnp.arange(part_count, dtype=jnp.int32)
     row_ids = (my_row + jnp.arange(ROWS, dtype=jnp.int32)) % ROWS
     groups = row_ids * plane + my_place
@@ -466,22 +492,6 @@
     my_part = row_parts[0]
     len_x = box_sizes[my_part, 0]
     len_y = box_sizes[my_part, 1]
-    table_x = cosine_table(N, len_x)
-    table_y = cosine_table(N, len_y)
-    table_z = cosine_table(N, jnp.int32(N))
-    tables = jnp.stack([table_x, table_x.T, table_y, table_y.T, table_z.T, table_z])
-    my_modes = lax.dynamic_slice_in_dim(table_y, my_column * X, X, 0)
-    my_face = jnp.concatenate(
-        [my_modes[:, 0:3], lax.dynamic_slice_in_dim(my_modes, len_y - 3, 3, 1)], axis=1
-    )
-    count = jnp.arange(N, dtype=jnp.int32).astype(f32)
-    quarter = f32((jnp.pi * time_step / 2) ** 2)
-    square_x = quarter * (count / len_x.astype(f32)) ** 2
-    square_z = quarter * (count / f32(N)) ** 2
-    mode_y = (my_column * X + jnp.arange(X, dtype=jnp.int32)).astype(f32)
-    square_y = quarter * (mode_y / len_y.astype(f32)) ** 2
-    base = square_x[:, None] + square_z[None, :]
-    floats = jnp.concatenate([square_y, my_face.reshape(-1)])
     item_ids = jnp.arange(item_count, dtype=jnp.int32)
     link_ids = partner[row_parts].reshape(ROWS, item_count)
     safe_links = jnp.maximum(link_ids, 0)
@@ -491,10 +501,10 @@
     shift = (item_ids[None, :] % seg_count - peer_seg) % seg_count
     here = (peer_group // plane == my_row) & (link_ids >= 0)
     picks = jnp.stack([peer_group % plane, shift, here.astype(jnp.int32)], axis=-1)
-    ints = jnp.concatenate([jnp.stack([len_x, len_y]), picks.reshape(-1)])
+    picks = jnp.concatenate([picks.reshape(-1), jnp.stack([len_x, len_y])])
     x_limit = jnp.where(link_ids[0] >= 0, jnp.minimum(len_x, box_sizes[peer_part[0], 0]), 0)
-    limits = jnp.repeat(x_limit.reshape(2, seg_count), N // seg_count, axis=1).astype(f32)
-    limits = jnp.concatenate([limits, jnp.zeros((6, N), f32)], axis=0)
+    limits = jnp.repeat(x_limit.reshape(2, seg_count), N // seg_count, axis=1)
+    limits = jnp.concatenate([limits, jnp.zeros((6, N), jnp.int32)], axis=0)
 
     vmem = pl.BlockSpec(memory_space=pltpu.VMEM)
     smem = pl.BlockSpec(memory_space=pltpu.SMEM)
@@ -504,7 +514,7 @@
     return pl.pallas_call(
         kernel,
         out_shape=(block, block),
-        in_specs=[smem, smem, anywhere, anywhere, vmem, vmem, vmem],
+        in_specs=[smem, vmem, anywhere, anywhere],
         out_specs=(anywhere, anywhere),
         scratch_shapes=[
             pltpu.VMEM((2, X, N, N), f32),
@@ -513,14 +523,16 @@
             pltpu.VMEM((2, N, X, N), f32),
             pltpu.VMEM((2, X, N, N), f32),
             pltpu.VMEM((6, 2 * N, 2 * N), bf16),
+            pltpu.VMEM((N, N), f32),
+            pltpu.VMEM((8 * X, N), f32),
             pltpu.VMEM((2, X, N, N), f32),
             pltpu.VMEM((X, N, N), f32),
             pltpu.VMEM((X, N, N), f32),
             pltpu.VMEM((6, N, N), f32),
             pltpu.VMEM((2, 6, N, N), f32),
             pltpu.VMEM((2, 3, 6, X, N), f32),
-            pltpu.VMEM((plane, 6, X, N), f32),
-            pltpu.VMEM((plane, 6, X, N), f32),
+            pltpu.VMEM((RING * CORES, 6, X, N), f32),
+            pltpu.VMEM((RING * CORES, 6, X, N), f32),
             pltpu.VMEM((2, ROWS, 6, X, N), f32),
             pltpu.VMEM((2, 3, 6, X, N), f32),
             pltpu.VMEM((2, 6, X, N), f32),
@@ -547,7 +559,7 @@
             collective_id=0, has_side_effects=True, vmem_limit_bytes=64 * 1000 * 1000
         ),
         name="two_steps",
-    )(ints, floats, adj_next, adj_later, tables, base, limits)
+    )(picks, limits, adj_next, adj_later)
 
 
 def solution(mesh):

time: 156 us -> 147 us (0.942)
  other arithmetic: 8.5 us -> 3.66 us
  between operations: 3.71 us -> 0.85 us
    unnamed x9 -> x7, local copies, waits for them, and re-layouts: 6.15 us -> 5.41 us
where the time goes in v2:
time: 147 us; the launch traced here: 145 us
  Pallas kernels  129 us (88%)
  local copies, waits for them, and re-layouts  11.5 us (8%)
  other arithmetic  3.66 us (2%)
    pallas_call x1, Pallas kernels, local(): pl.pallas_call(kernel, out_shape=(block, block), in_specs=[smem, vmem, an...  129 us
    unnamed x7, local copies, waits for them, and re-layouts  5.41 us

profile of v2, /device:TPU:9, one launch (start us, length us, event | category | flops | bytes accessed | tf_op | source)
XLA Modules:
  0.0 144.5 jit_solution(8739261340816008476)
XLA Ops:
  0.6 0.0 copy-start
  0.7 0.9 select_reduce_fusion
  1.7 1.4 constant_dynamic-slice_fusion.1
  3.1 0.8 copy.42
  3.9 0.6 gather_fusion
  4.5 0.1 copy.57
  4.6 0.1 copy.43
  4.7 0.1 copy.55
  4.8 0.1 copy.60
  4.9 0.1 copy.61
  5.0 0.1 add_select_fusion.2
  5.1 0.1 copy.47
  5.2 0.1 reshape.336
  5.3 0.1 slice_reduce_fusion
  5.4 1.3 gather_fusion.2
  6.7 0.7 broadcast_minimum_fusion
  7.4 0.1 min.12
  7.5 0.1 broadcast_in_dim.18
  7.5 0.1 reshape.325
  7.6 0.6 concatenate.11.limits
  8.2 0.0 copy-done
  8.2 0.7 gather_fusion.1
  8.9 0.1 gather.13
  9.0 0.1 copy.48
  9.2 0.1 copy.56
  9.3 0.1 reshape.324
  9.4 1.9 %pad_add_fusion.1.picks = s32[98]{0:T(128)} fusion(s32[1]{0:T(128)} %bitcast.8, s32[1]{0:T(128)} %bitcast.7, s32[96]{0:T(128)S(1)} %reshape.324), kind=kLoop, calls=%fused_computation.47 | loop fusion | flops 196 | bytes 784 | tf_op jit(solution)/shard_map/concatenate | solution.py:504
  11.4 128.6 %two_steps.1 = (f32[1,32,128,128]{3,2,1,0:T(8,128)}, f32[1,32,128,128]{3,2,1,0:T(8,128)}) custom-call(s32[98]{0:T(128)} %pad_add_fusion.1.picks, s32[8,128]{1,0:T(8,128)} %concatenate.11.limits, f32[1,32,128,128]{3,2,1,0:T(8,128)} %adj_next.1, f32[1,32,128,128]{3,2,1,0:T(8,128)} %adj_later.1), custom_call_target="tpu_custom_call" | custom-call | tf_op jit(solution)/shard_map/two_steps/pallas_call | solution.py:514
  139.9 0.0 copy-start.1
  139.9 3.3 %copy.65 = f32[1,32,128,128]{3,2,1,0:T(8,128)} copy(f32[1,32,128,128]{3,2,1,0:T(8,128)} %get-tuple-element.13) | data formatting | bytes 4194304
  143.2 0.0 copy-done.1
  143.2 1.3 copy.66
  (13 shorter events, 0.1 us)
Async XLA Ops:
  0.6 7.6 %copy-start = (s32[64]{0:T(128)S(1)}, s32[64]{0:T(128)}, u32[]{:S(2)}) copy-start(s32[64]{0:T(128)} %param.8) | copy-start | bytes 772
  139.9 3.3 %copy-start.1 = (f32[1,32,128,128]{3,2,1,0:T(8,128)S(1)}, f32[1,32,128,128]{3,2,1,0:T(8,128)}, u32[]{:S(2)}) copy-start(f32[1,32,128,128]{3,2,1,0:T(8,128)} %get-tuple-element.14) | copy-start | bytes 6291460

commit v3 on v2

--- a/solution.py
+++ b/solution.py
@@ -256,8 +256,9 @@
         fill = list(fill)
 
         def other_work():
-            if fill:
-                fill.pop(0)()
+            work = fill.pop(0) if fill else None
+            if work:
+                work()
 
         other_work()
         for j in (1, 3, 2):
@@ -303,7 +304,8 @@
         for j in (2, 1, 3):
             post(row_copy(e, j))
         for work in fill:
-            work()
+            if work:
+                work()
         for j in (1, 3, 2):
             row_copy(e, j).wait_recv()
         other = wanted[e, 0] + wanted_in[e, 0] + wanted_in[e, 1] + wanted_in[e, 2]
@@ -409,7 +411,7 @@
 
     exchange(
         0,
-        [start(1, 2), start(1, 3), start(2, 0), start(2, 1), start(2, 2), start(2, 3), later_modes],
+        [start(1, 2), None, start(1, 3), None, start(2, 0), start(2, 1), later_modes],
     )
 
     def all_copy(j):
@@ -426,6 +428,7 @@
     coup_all[:, pl.ds(X * sub, X), :] = coup_rows
     for j in (2, 1, 3):
         post(all_copy(j))
+    large_start(2, 2)
     for r in range(6):
         faces[r] = jnp.zeros((N, N), f32)
     for j in (1, 3, 2):
@@ -458,6 +461,7 @@
         return carry
 
     lax.fori_loop(0, X // 2, second_back, 0, unroll=2)
+    large_start(2, 3)
     for c in range(CHUNKS):
         large_start(3, c)
 
@@ -468,7 +472,7 @@
 
         return work
 
-    exchange(1, [finish(0, 0), finish(0, 1), finish(0, 2), finish(0, 3)])
+    exchange(1, [None, finish(0, 0), finish(0, 1), finish(0, 2), finish(0, 3)])
     for c in range(CHUNKS):
         finish(1, c)()
     for copy in sent:
@@ -478,37 +482,55 @@
             store(i, c).wait()
 
 
+def plan_kernel(box_sizes, holder, partner, picks, limits):
+    row, core, sub = lax.axis_index("row"), lax.axis_index("core"), lax.axis_index("sub")
+    plane = RING * CORES
+    place = lax.axis_index("z") * CORES + core
+
+    def find(i, found):
+        group = holder[i]
+        return tuple(
+            jnp.where(group == lax.rem(row + j, ROWS) * plane + place, i, found[j]) for j in range(ROWS)
+        )
+
+    row_parts = lax.fori_loop(0, holder.shape[0], find, (jnp.int32(0),) * ROWS, unroll=8)
+    len_x, len_y = box_sizes[0, row_parts[0]], box_sizes[1, row_parts[0]]
+    picks[96] = len_x
+    picks[97] = len_y
+    for j in range(ROWS):
+        for item in range(8):
+            link = partner[item // 4, item % 4, row_parts[j]]
+            target = jnp.maximum(link, 0)
+            group = holder[target >> 2]
+            at = 3 * (8 * j + item)
+            picks[at] = group & (plane - 1)
+            picks[at + 1] = (item - target) & 3
+            picks[at + 2] = jnp.where((link >= 0) & ((group >> 4) == row), 1, 0)
+    face = lax.broadcasted_iota(jnp.int32, (8, N), 0)
+    seg = lax.broadcasted_iota(jnp.int32, (8, N), 1) >> 5
+    values = jnp.zeros((8, N), jnp.int32)
+    for item in range(8):
+        link = partner[item // 4, item % 4, row_parts[0]]
+        limit = jnp.minimum(len_x, box_sizes[0, jnp.maximum(link, 0) >> 2])
+        here = (face == item // 4) & (seg == item % 4)
+        values = jnp.where(here, jnp.where(link >= 0, limit, 0), values)
+    limits[...] = values
+
+
 def local(adj_next, adj_later, box_sizes, holder, partner):
-    part_count = holder.shape[0]
-    seg_count = partner.shape[2]
-    item_count = 2 * seg_count
-    plane = RING * CORES
-    my_row = lax.axis_index("row")
-    my_place = lax.axis_index("z") * CORES + lax.axis_index("core")
-    part_ids = jnp.arange(part_count, dtype=jnp.int32)
-    row_ids = (my_row + jnp.arange(ROWS, dtype=jnp.int32)) % ROWS
-    groups = row_ids * plane + my_place
-    row_parts = jnp.sum(jnp.where(holder[None, :] == groups[:, None], part_ids[None, :], 0), axis=1)
-    my_part = row_parts[0]
-    len_x = box_sizes[my_part, 0]
-    len_y = box_sizes[my_part, 1]
-    item_ids = jnp.arange(item_count, dtype=jnp.int32)
-    link_ids = partner[row_parts].reshape(ROWS, item_count)
-    safe_links = jnp.maximum(link_ids, 0)
-    peer_part = safe_links // seg_count
-    peer_seg = safe_links % seg_count
-    peer_group = holder[peer_part]
-    shift = (item_ids[None, :] % seg_count - peer_seg) % seg_count
-    here = (peer_group // plane == my_row) & (link_ids >= 0)
-    picks = jnp.stack([peer_group % plane, shift, here.astype(jnp.int32)], axis=-1)
-    picks = jnp.concatenate([picks.reshape(-1), jnp.stack([len_x, len_y])])
-    x_limit = jnp.where(link_ids[0] >= 0, jnp.minimum(len_x, box_sizes[peer_part[0], 0]), 0)
-    limits = jnp.repeat(x_limit.reshape(2, seg_count), N // seg_count, axis=1)
-    limits = jnp.concatenate([limits, jnp.zeros((6, N), jnp.int32)], axis=0)
-
     vmem = pl.BlockSpec(memory_space=pltpu.VMEM)
     smem = pl.BlockSpec(memory_space=pltpu.SMEM)
     anywhere = pl.BlockSpec(memory_space=pl.ANY)
+    picks, limits = pl.pallas_call(
+        plan_kernel,
+        out_shape=(
+            jax.ShapeDtypeStruct((128,), jnp.int32),
+            jax.ShapeDtypeStruct((8, N), jnp.int32),
+        ),
+        in_specs=[smem, smem, smem],
+        out_specs=(smem, vmem),
+        name="plan",
+    )(box_sizes.T, holder, jnp.transpose(partner, (1, 2, 0)))
     block = jax.ShapeDtypeStruct((1, X, N, N), f32)
     dma = pltpu.SemaphoreType.DMA
     return pl.pallas_call(

time: 147 us -> 131 us (0.89); the launches traced: 145 us -> 131 us
  local copies, waits for them, and re-layouts: 11.5 us -> 4.61 us
  other arithmetic: 3.66 us -> 0 us
  Pallas kernels: 129 us -> 126 us
    pallas_call x1, Pallas kernels: 129 us -> 124 us  [local(): pl.pallas_call(kernel, out_shape=(block, block), in_specs=[smem, vmem, an...]
    gather x5 -> x0, local copies, waits for them, and re-layouts: 2.77 us -> none  [the longest x1 1.33 us: local(): box_sizes[peer_part[0], 0]]
    concatenate x2 -> x0, other arithmetic: 1.96 us -> none  [the longest x1 1.95 us: local(): picks = jnp.concatenate([picks.reshape(-1), jnp.stack([len_x, len_y])])]
    pallas_call x0 -> x1, Pallas kernels: none -> 1.88 us  [local(): pl.pallas_call(plan_kernel, out_shape=(jax.ShapeDtypeStruct((128,), jnp.i...]
    unnamed x7 -> x4, local copies, waits for them, and re-layouts: 5.41 us -> 4.61 us
where the time goes in v3:
time: 131 us
  Pallas kernels  126 us (96%)
  local copies, waits for them, and re-layouts  4.61 us (4%)
    pallas_call x1, Pallas kernels, local(): pl.pallas_call(kernel, out_shape=(block, block), in_specs=[smem, vmem, an...  124 us
    unnamed x4, local copies, waits for them, and re-layouts  4.61 us

profile of v3, /device:TPU:9, one launch (start us, length us, event | category | flops | bytes accessed | tf_op | source)
XLA Modules:
  0.0 131.2 jit_solution(1327928720637896015)
XLA Ops:
  0.6 1.9 %plan.1 = (s32[128]{0:T(128)}, s32[8,128]{1,0:T(8,128)}) custom-call(s32[2,64]{1,0:T(2,128)} %bitcast.3, s32[64]{0:T(128)} %holder.1, s32[2,4,64]{2,1,0:T(4,128)} %bitcast.2), custom_call_target="tpu_custom_call" | custom-call | tf_op jit(solution)/shard_map/plan/pallas_call | solution.py:524
  2.5 124.1 %two_steps.1 = (f32[1,32,128,128]{3,2,1,0:T(8,128)}, f32[1,32,128,128]{3,2,1,0:T(8,128)}) custom-call(s32[128]{0:T(128)} %get-tuple-element.4.picks, s32[8,128]{1,0:T(8,128)} %get-tuple-element.5.limits, f32[1,32,128,128]{3,2,1,0:T(8,128)} %adj_next.1, f32[1,32,128,128]{3,2,1,0:T(8,128)} %adj_later.1), custom_call_target="tpu_custom_call" | custom-call | tf_op jit(solution)/shard_map/two_steps/pallas_call | solution.py:536
  126.6 0.0 copy-start
  126.6 3.3 %copy.9 = f32[1,32,128,128]{3,2,1,0:T(8,128)} copy(f32[1,32,128,128]{3,2,1,0:T(8,128)} %get-tuple-element.8) | data formatting | bytes 4194304
  129.9 0.0 copy-done
  129.9 1.3 %copy.10 = f32[1,32,128,128]{3,2,1,0:T(8,128)} copy(f32[1,32,128,128]{3,2,1,0:T(8,128)S(1)} %copy-done) | data formatting | bytes 4194304
Async XLA Ops:
  126.6 3.3 %copy-start = (f32[1,32,128,128]{3,2,1,0:T(8,128)S(1)}, f32[1,32,128,128]{3,2,1,0:T(8,128)}, u32[]{:S(2)}) copy-start(f32[1,32,128,128]{3,2,1,0:T(8,128)} %get-tuple-element.9) | copy-start | bytes 6291460

commit v4 on v3

--- a/solution.py
+++ b/solution.py
@@ -324,7 +324,23 @@
     y_index = down
     face_rows = [0, 1, 2, len_y - 3, len_y - 2, len_y - 1]
 
-    def finish_chunk(i, c):
+    def coupling_rows(i, x):
+        extra = jnp.zeros((N, N), f32)
+        for r in range(6):
+            line = jnp.broadcast_to(coup[i, r, pl.ds(x, 1), :], (N, N))
+            extra = jnp.where(y_index == face_rows[r], line, extra)
+        return extra
+
+    def add_coupling(i, c):
+        def step(p, carry):
+            x = CX * c + p
+            land[i, x] = land[i, x] + coupling_rows(i, x)
+            return carry
+
+        lax.fori_loop(0, CX, step, 0, unroll=2)
+        store(i, c).start()
+
+    def finish_chunk(i, c, coupled):
         def step(p, carry):
             x0 = CX * c + 2 * p
             value = left_times(stacks[3], jnp.concatenate([land[i, x0], land[i, x0 + 1]], 1))
@@ -334,15 +350,12 @@
                 result = value[N * q : N * q + N]
                 inside = (y_index < len_y) & (jnp.full((N, N), sub * X + x, jnp.int32) < len_x)
                 result = result - jnp.where(inside, fields[1 - i, x], 0.0)
-                extra = jnp.zeros((N, N), f32)
-                for r in range(6):
-                    line = jnp.broadcast_to(coup[i, r, pl.ds(x, 1), :], (N, N))
-                    extra = jnp.where(y_index == face_rows[r], line, extra)
-                land[i, x] = result + extra
+                land[i, x] = result + coupling_rows(i, x) if coupled else result
             return carry
 
         lax.fori_loop(0, CX // 2, step, 0, unroll=2)
-        store(i, c).start()
+        if coupled:
+            store(i, c).start()
 
     def store(i, c):
         return pltpu.make_async_copy(
@@ -465,16 +478,21 @@
     for c in range(CHUNKS):
         large_start(3, c)
 
-    def finish(i, c):
+    def finish(i, c, coupled=True):
         def work():
             large_wait(2 + i, c)
-            finish_chunk(i, c)
+            finish_chunk(i, c, coupled)
 
         return work
 
-    exchange(1, [None, finish(0, 0), finish(0, 1), finish(0, 2), finish(0, 3)])
-    for c in range(CHUNKS):
-        finish(1, c)()
+    exchange(
+        1,
+        [None, finish(0, 0), finish(0, 1), finish(0, 2), finish(0, 3), None, finish(1, 0, False), finish(1, 1, False)],
+    )
+    add_coupling(1, 0)
+    add_coupling(1, 1)
+    finish(1, 2)()
+    finish(1, 3)()
     for copy in sent:
         copy.wait_send()
     for i in range(2):

time: 131 us -> 130 us (level)
  Pallas kernels: 126 us -> 124 us
    pallas_call x1, Pallas kernels: 124 us -> 123 us  [local(): pl.pallas_call(kernel, out_shape=(block, block), in_specs=[smem, vmem, an...]
where the time goes in v4:
time: 130 us
  Pallas kernels  124 us (95%)
  local copies, waits for them, and re-layouts  4.61 us (4%)
    pallas_call x1, Pallas kernels, local(): pl.pallas_call(kernel, out_shape=(block, block), in_specs=[smem, vmem, an...  123 us
    unnamed x4, local copies, waits for them, and re-layouts  4.61 us

profile of v4, /device:TPU:9, one launch (start us, length us, event | category | flops | bytes accessed | tf_op | source)
XLA Modules:
  0.0 129.7 jit_solution(5618551489122802544)
XLA Ops:
  0.6 1.9 %plan.1 = (s32[128]{0:T(128)}, s32[8,128]{1,0:T(8,128)}) custom-call(s32[2,64]{1,0:T(2,128)} %bitcast.3, s32[64]{0:T(128)} %holder.1, s32[2,4,64]{2,1,0:T(4,128)} %bitcast.2), custom_call_target="tpu_custom_call" | custom-call | tf_op jit(solution)/shard_map/plan/pallas_call | solution.py:542
  2.5 122.5 %two_steps.1 = (f32[1,32,128,128]{3,2,1,0:T(8,128)}, f32[1,32,128,128]{3,2,1,0:T(8,128)}) custom-call(s32[128]{0:T(128)} %get-tuple-element.4.picks, s32[8,128]{1,0:T(8,128)} %get-tuple-element.5.limits, f32[1,32,128,128]{3,2,1,0:T(8,128)} %adj_next.1, f32[1,32,128,128]{3,2,1,0:T(8,128)} %adj_later.1), custom_call_target="tpu_custom_call" | custom-call | tf_op jit(solution)/shard_map/two_steps/pallas_call | solution.py:554
  125.1 0.0 copy-start
  125.1 3.3 %copy.9 = f32[1,32,128,128]{3,2,1,0:T(8,128)} copy(f32[1,32,128,128]{3,2,1,0:T(8,128)} %get-tuple-element.8) | data formatting | bytes 4194304
  128.4 0.0 copy-done
  128.4 1.3 %copy.10 = f32[1,32,128,128]{3,2,1,0:T(8,128)} copy(f32[1,32,128,128]{3,2,1,0:T(8,128)S(1)} %copy-done) | data formatting | bytes 4194304
Async XLA Ops:
  125.1 3.3 %copy-start = (f32[1,32,128,128]{3,2,1,0:T(8,128)S(1)}, f32[1,32,128,128]{3,2,1,0:T(8,128)}, u32[]{:S(2)}) copy-start(f32[1,32,128,128]{3,2,1,0:T(8,128)} %get-tuple-element.9) | copy-start | bytes 6291460

commit v5 on v4

--- a/solution.py
+++ b/solution.py
@@ -300,9 +300,10 @@
                 wanted[e, j, 3 * face : 3 * face + 3] = total
             return carry
 
-        lax.fori_loop(0, ROWS, choose, 0)
         for j in (2, 1, 3):
+            choose(j, 0)
             post(row_copy(e, j))
+        choose(0, 0)
         for work in fill:
             if work:
                 work()

time: 130 us -> 130 us (level); the launches traced: 130 us -> 128 us
    pallas_call x1, Pallas kernels: 123 us -> 121 us  [local(): pl.pallas_call(kernel, out_shape=(block, block), in_specs=[smem, vmem, an...]
where the time goes in v5:
time: 130 us; the launch traced here: 128 us
  Pallas kernels  123 us (95%)
  local copies, waits for them, and re-layouts  4.61 us (4%)
    pallas_call x1, Pallas kernels, local(): pl.pallas_call(kernel, out_shape=(block, block), in_specs=[smem, vmem, an...  121 us
    unnamed x4, local copies, waits for them, and re-layouts  4.61 us

profile of v5, /device:TPU:9, one launch (start us, length us, event | category | flops | bytes accessed | tf_op | source)
XLA Modules:
  0.0 127.8 jit_solution(12043910378152581458)
XLA Ops:
  0.6 1.9 %plan.1 = (s32[128]{0:T(128)}, s32[8,128]{1,0:T(8,128)}) custom-call(s32[2,64]{1,0:T(2,128)} %bitcast.3, s32[64]{0:T(128)} %holder.1, s32[2,4,64]{2,1,0:T(4,128)} %bitcast.2), custom_call_target="tpu_custom_call" | custom-call | tf_op jit(solution)/shard_map/plan/pallas_call | solution.py:543
  2.5 120.7 %two_steps.1 = (f32[1,32,128,128]{3,2,1,0:T(8,128)}, f32[1,32,128,128]{3,2,1,0:T(8,128)}) custom-call(s32[128]{0:T(128)} %get-tuple-element.4.picks, s32[8,128]{1,0:T(8,128)} %get-tuple-element.5.limits, f32[1,32,128,128]{3,2,1,0:T(8,128)} %adj_next.1, f32[1,32,128,128]{3,2,1,0:T(8,128)} %adj_later.1), custom_call_target="tpu_custom_call" | custom-call | tf_op jit(solution)/shard_map/two_steps/pallas_call | solution.py:555
  123.2 0.0 copy-start
  123.2 3.3 %copy.9 = f32[1,32,128,128]{3,2,1,0:T(8,128)} copy(f32[1,32,128,128]{3,2,1,0:T(8,128)} %get-tuple-element.8) | data formatting | bytes 4194304
  126.5 0.0 copy-done
  126.5 1.3 %copy.10 = f32[1,32,128,128]{3,2,1,0:T(8,128)} copy(f32[1,32,128,128]{3,2,1,0:T(8,128)S(1)} %copy-done) | data formatting | bytes 4194304
Async XLA Ops:
  123.2 3.3 %copy-start = (f32[1,32,128,128]{3,2,1,0:T(8,128)S(1)}, f32[1,32,128,128]{3,2,1,0:T(8,128)}, u32[]{:S(2)}) copy-start(f32[1,32,128,128]{3,2,1,0:T(8,128)} %get-tuple-element.9) | copy-start | bytes 6291460
